TPU v7x, 32 devices: a whole 2x2x4 slice. The times are simulated.
32 devices in a mesh: batch: 4 (over z), pb: 2 (over x), ka: 4 (over y, core).
Axes of the slice: x: 2, y: 2, z: 4, core: 2. Of those that a mesh axis runs over, the one named last changes fastest.
Arguments:
- inputs: bfloat16 [16, 1024, 768], P('batch', ('pb', 'ka')), may hold values from -6 to 6
- block_place: int32 [16, 8], P('batch'), may hold values from 0 to 7, each once within a row
- ln1_gain: float32 [768], replicated, may hold values from 0.1 to 1.9
- ln1_shift: float32 [768], replicated, may hold values from -3 to 3
- w_qkv: bfloat16 [768, 2304], replicated, may hold values from -0.21875 to 0.21875
- w_out: bfloat16 [768, 768], replicated, may hold values from -1.25 to 1.25
- ln2_gain: float32 [768], replicated, may hold values from 0.1 to 1.9
- ln2_shift: float32 [768], replicated, may hold values from -3 to 3
- w_up: bfloat16 [768, 3072], replicated, may hold values from -0.21875 to 0.21875
- w_down: bfloat16 [3072, 768], replicated, may hold values from -0.109375 to 0.109375
- cotangent: bfloat16 [16, 1024, 768], P('batch', ('pb', 'ka')), may hold values from -6 to 6
Outputs:
- outputs: bfloat16 [16, 1024, 768], P('batch', ('pb', 'ka'))
- grad_inputs: bfloat16 [16, 1024, 768], P('batch', ('pb', 'ka'))
- grad_qkv: float32 [768, 2304], P('batch', ('pb', 'ka'))
- grad_proj: float32 [768, 768], P('batch', ('pb', 'ka'))
- grad_up: float32 [768, 3072], P('batch', ('pb', 'ka'))
- grad_down: float32 [3072, 768], P('batch', ('pb', 'ka'))
- grad_norms: float32 [4, 768], P(None, ('pb', 'ka'))
Inputs may be any that keep to these rules, and one draw needn't show every extreme that they name: Each row of block_place lists every number 0 to 7 exactly once.
All inputs are finite; a program needn't handle non-finite values.
Results may differ from a plain program's by a relative error of at most 0.015.
The roundings to bfloat16 on the way count: a program that leaves them out, or rounds other values in their place, can miss the bound.
Values may be sent and summed in bfloat16 or wider, within the bound.
No kernel may reach another device: no remote copies, remote signals or barrier semaphores. Data moves between devices by JAX's collectives and lax.ppermute only.
A program may use at most 192 MiB of HBM per device.

v0:
```python
import jax
import jax.numpy as jnp
from jax import lax
from jax.sharding import PartitionSpec as P

HEADS = 12
HEAD = 64
norm_eps = 1e-05


def merged(part, axis, combine):
    gathered = jax.tree.map(lambda a: lax.all_gather(a, axis), part)

    def take(source):
        return jax.tree.map(lambda a: lax.dynamic_index_in_dim(a, source, 0, False), gathered)

    return lax.fori_loop(
        1, lax.axis_size(axis), lambda source, state: combine(state, take(source)), take(0)
    )


def norm_rows(values, gain_vec, shift_vec):
    average = jnp.mean(values, axis=-1, keepdims=True)
    centred = values - average
    spread = jnp.mean(centred * centred, axis=-1, keepdims=True)
    return centred * lax.rsqrt(spread + norm_eps) * gain_vec + shift_vec


def gelu_tanh(values):
    return jax.nn.gelu(values, approximate=True)


def split_heads(matrix):
    return matrix.reshape(matrix.shape[0], matrix.shape[1], HEADS, HEAD)


def combine_stats(former, latter):
    largest = jnp.maximum(former[0], latter[0])
    return (
        largest,
        former[1] * jnp.exp(former[0] - largest) + latter[1] * jnp.exp(latter[0] - largest),
    )


def tile_scores(query_heads, key_heads):
    return HEAD ** (-0.5) * jnp.einsum(
        "bqhe,bkhe->bhqk", query_heads, key_heads, preferred_element_type=jnp.float32
    )


def tile_weights(scores, visible, row_peak, row_total):
    sign_part = jnp.sign(scores)
    prob_part = (
        jnp.exp(jnp.where(visible, jnp.abs(scores) - row_peak[..., None], -1e30))
        / row_total[..., None]
    )
    return (sign_part, prob_part, sign_part * prob_part)


def shards(
    inputs,
    block_place,
    ln1_gain,
    ln1_shift,
    w_qkv,
    w_out,
    ln2_gain,
    ln2_shift,
    w_up,
    w_down,
    cotangent,
):
    seq_count, block_rows, model_width = inputs.shape
    key_devices = lax.axis_size("ka")
    query_devices = lax.axis_size("pb")
    query_index = lax.axis_index("pb")
    key_index = lax.axis_index("ka")
    offsets = jnp.arange(block_rows, dtype=jnp.int32)
    query_slots = query_index * key_devices + jnp.arange(key_devices, dtype=jnp.int32)
    key_slots = key_index + key_devices * jnp.arange(query_devices, dtype=jnp.int32)
    query_pos = (
        jnp.take(block_place, query_slots, axis=1)[:, :, None] * block_rows + offsets[None, None, :]
    ).reshape(seq_count, key_devices * block_rows)
    key_pos = (
        jnp.take(block_place, key_slots, axis=1)[:, :, None] * block_rows + offsets[None, None, :]
    ).reshape(seq_count, query_devices * block_rows)
    visible = key_pos[:, None, None, :] <= query_pos[:, None, :, None]
    source = inputs.astype(jnp.float32)
    normed1, first_back = jax.vjp(norm_rows, source, ln1_gain, ln1_shift)
    normed1 = normed1.astype(jnp.bfloat16)
    packed = jnp.einsum("btd,de->bte", normed1, w_qkv, preferred_element_type=jnp.float32).astype(
        jnp.bfloat16
    )
    query_half = lax.all_gather(packed[..., :model_width], "ka", axis=1, tiled=True)
    key_set, value_set = (
        lax.all_gather(packed[..., model_width : 2 * model_width], "pb", axis=1, tiled=True),
        lax.all_gather(packed[..., 2 * model_width :], "pb", axis=1, tiled=True),
    )
    query_heads = split_heads(query_half)
    key_heads = split_heads(key_set)
    value_heads = split_heads(value_set)
    scores = tile_scores(query_heads, key_heads)
    magnitude = jnp.abs(scores)
    local_peak = jnp.max(jnp.where(visible, magnitude, -1e30), axis=-1)
    local_sum = jnp.sum(
        jnp.exp(jnp.where(visible, magnitude - local_peak[..., None], -1e30)), axis=-1
    )
    row_peak, row_total = merged((local_peak, local_sum), "ka", combine_stats)
    sign_part, prob_part, signed = tile_weights(scores, visible, row_peak, row_total)
    weights_low = signed.astype(jnp.bfloat16)
    partial_value = jnp.einsum(
        "bhqk,bkhe->bqhe", weights_low, value_heads, preferred_element_type=jnp.float32
    )
    partial_value = partial_value.reshape(seq_count, key_devices * block_rows, model_width)
    attended = lax.psum_scatter(partial_value, "ka", scatter_dimension=1, tiled=True).astype(
        jnp.bfloat16
    )
    residual = source + jnp.einsum(
        "btd,de->bte", attended, w_out, preferred_element_type=jnp.float32
    )
    normed2, second_back = jax.vjp(norm_rows, residual, ln2_gain, ln2_shift)
    normed2 = normed2.astype(jnp.bfloat16)
    pre_act = jnp.einsum("btd,df->btf", normed2, w_up, preferred_element_type=jnp.float32)
    active, gelu_back = jax.vjp(gelu_tanh, pre_act)
    active = active.astype(jnp.bfloat16)
    outputs = (
        residual + jnp.einsum("btf,fd->btd", active, w_down, preferred_element_type=jnp.float32)
    ).astype(jnp.bfloat16)
    grad_down = jnp.einsum("btf,btd->fd", active, cotangent, preferred_element_type=jnp.float32)
    grad_act = jnp.einsum("btd,fd->btf", cotangent, w_down, preferred_element_type=jnp.float32)
    grad_pre = gelu_back(grad_act)[0].astype(jnp.bfloat16)
    grad_up = jnp.einsum("btd,btf->df", normed2, grad_pre, preferred_element_type=jnp.float32)
    grad_normed2 = jnp.einsum("btf,df->btd", grad_pre, w_up, preferred_element_type=jnp.float32)
    grad_res, grad_gain2, grad_shift2 = second_back(grad_normed2)
    grad_res = grad_res + cotangent.astype(jnp.float32)
    grad_z = grad_res.astype(jnp.bfloat16)
    grad_proj = jnp.einsum("btd,bte->de", attended, grad_z, preferred_element_type=jnp.float32)
    grad_att = jnp.einsum("bte,de->btd", grad_z, w_out, preferred_element_type=jnp.float32).astype(
        jnp.bfloat16
    )
    grad_half = lax.all_gather(grad_att, "ka", axis=1, tiled=True)
    grad_heads = split_heads(grad_half)
    scores = tile_scores(query_heads, key_heads)
    sign_part, prob_part, signed = tile_weights(scores, visible, row_peak, row_total)
    weights_low = signed.astype(jnp.bfloat16)
    grad_weights = jnp.einsum(
        "bqhe,bkhe->bhqk", grad_heads, value_heads, preferred_element_type=jnp.float32
    )
    delta_rows = lax.psum(jnp.sum(signed * grad_weights, axis=-1), "ka")
    grad_scores = (
        sign_part * prob_part * (sign_part * grad_weights - delta_rows[..., None])
    ).astype(jnp.bfloat16)
    factor = HEAD ** (-0.5)
    grad_q = factor * jnp.einsum(
        "bhqk,bkhe->bqhe", grad_scores, key_heads, preferred_element_type=jnp.float32
    )
    grad_k = factor * jnp.einsum(
        "bhqk,bqhe->bkhe", grad_scores, query_heads, preferred_element_type=jnp.float32
    )
    grad_v = jnp.einsum(
        "bhqk,bqhe->bkhe", weights_low, grad_heads, preferred_element_type=jnp.float32
    )
    query_grad = lax.psum_scatter(
        grad_q.reshape(seq_count, key_devices * block_rows, model_width).astype(jnp.bfloat16),
        "ka",
        scatter_dimension=1,
        tiled=True,
    ).astype(jnp.float32)
    key_grad, value_grad = (
        lax.psum_scatter(
            grad_k.reshape(seq_count, query_devices * block_rows, model_width).astype(jnp.bfloat16),
            "pb",
            scatter_dimension=1,
            tiled=True,
        ).astype(jnp.float32),
        lax.psum_scatter(
            grad_v.reshape(seq_count, query_devices * block_rows, model_width).astype(jnp.bfloat16),
            "pb",
            scatter_dimension=1,
            tiled=True,
        ).astype(jnp.float32),
    )
    grad_packed = jnp.concatenate([query_grad, key_grad, value_grad], axis=-1).astype(jnp.bfloat16)
    grad_qkv = jnp.einsum("btd,bte->de", normed1, grad_packed, preferred_element_type=jnp.float32)
    grad_normed1 = jnp.einsum("bte,de->btd", grad_packed, w_qkv, preferred_element_type=jnp.float32)
    grad_source, grad_gain1, grad_shift1 = first_back(grad_normed1)
    grad_inputs = (grad_res + grad_source).astype(jnp.bfloat16)
    norm_local = jnp.stack([grad_gain1, grad_shift1, grad_gain2, grad_shift2])
    widened = (
        lax.psum_scatter(
            grad_qkv.astype(jnp.bfloat16), "batch", scatter_dimension=0, tiled=True
        ).astype(jnp.float32),
        lax.psum_scatter(
            grad_proj.astype(jnp.bfloat16), "batch", scatter_dimension=0, tiled=True
        ).astype(jnp.float32),
        lax.psum_scatter(
            grad_up.astype(jnp.bfloat16), "batch", scatter_dimension=0, tiled=True
        ).astype(jnp.float32),
        lax.psum_scatter(
            grad_down.astype(jnp.bfloat16), "batch", scatter_dimension=0, tiled=True
        ).astype(jnp.float32),
    )
    summed = (
        lax.psum_scatter(
            widened[0].astype(jnp.bfloat16), ("pb", "ka"), scatter_dimension=1, tiled=True
        ).astype(jnp.float32),
        lax.psum_scatter(
            widened[1].astype(jnp.bfloat16), ("pb", "ka"), scatter_dimension=1, tiled=True
        ).astype(jnp.float32),
        lax.psum_scatter(
            widened[2].astype(jnp.bfloat16), ("pb", "ka"), scatter_dimension=1, tiled=True
        ).astype(jnp.float32),
        lax.psum_scatter(
            widened[3].astype(jnp.bfloat16), ("pb", "ka"), scatter_dimension=1, tiled=True
        ).astype(jnp.float32),
        lax.psum_scatter(
            norm_local.astype(jnp.bfloat16), ("pb", "ka"), scatter_dimension=1, tiled=True
        ).astype(jnp.float32),
    )
    norm_sum = lax.psum(summed[4], "batch")
    return (outputs, grad_inputs, summed[0], summed[1], summed[2], summed[3], norm_sum)


def solution(mesh):
    placed = (
        P("batch", ("pb", "ka"), None),
        P("batch", None),
        P(),
        P(),
        P(),
        P(),
        P(),
        P(),
        P(),
        P(),
        P("batch", ("pb", "ka"), None),
    )
    return jax.shard_map(
        shards,
        mesh=mesh,
        in_specs=placed,
        out_specs=(
            P("batch", ("pb", "ka"), None),
            P("batch", ("pb", "ka"), None),
            P("batch", ("pb", "ka")),
            P("batch", ("pb", "ka")),
            P("batch", ("pb", "ka")),
            P("batch", ("pb", "ka")),
            P(None, ("pb", "ka")),
        ),
        check_vma=False,
    )
```

profile of v0, /device:TPU:0, one launch (start us, length us, event | category | flops | bytes accessed | tf_op | source)
XLA Modules:
  0.0 959.3 jit_solution(2006295980375979858)
XLA Ops:
  10.8 3.3 convolution_convert_fusion
  20.1 25.6 %all-gather.11.cloned.1.call-done = bf16[4,256,768]{2,1,0:T(8,128)(2,1)} async-done(((bf16[4,128,768]{2,1,0:T(8,128)(2,1)}), bf16[4,256,768]{2,1,0:T(8,128)(2,1)}) %all-gather.11.cloned.1.call-update) | async-done | bytes 1572880 | tf_op jit(solution)/shard_map/all_gather | solution.py:96
  45.7 2.6 copy.64
  48.3 26.2 %all-gather.7.cloned.1.call-done = bf16[4,256,768]{2,1,0:T(8,128)(2,1)} async-done(((bf16[4,128,768]{2,1,0:T(8,128)(2,1)}), bf16[4,256,768]{2,1,0:T(8,128)(2,1)}) %all-gather.7.cloned.1.call-update) | async-done | bytes 1572880 | tf_op jit(solution)/shard_map/all_gather | solution.py:97
  74.5 2.6 copy.62
  77.0 28.1 %all-gather.9.cloned.1.call-done = bf16[4,512,768]{2,1,0:T(8,128)(2,1)} async-done(((bf16[4,128,768]{2,1,0:T(8,128)(2,1)}), bf16[4,512,768]{2,1,0:T(8,128)(2,1)}) %all-gather.9.cloned.1.call-update) | async-done | bytes 3145744 | tf_op jit(solution)/shard_map/all_gather | solution.py:94
  105.2 4.7 copy.63
  109.9 13.1 %select_reduce_fusion = (f32[4,12,512]{2,1,0:T(8,128)S(1)}, f32[4,12,512,256]{2,3,1,0:T(8,128)}) fusion(pred[4,512,256]{1,2,0:T(8,128)(4,1)} %broadcast_compare_fusion, bf16[4,512,12,64]{1,3,2,0:T(8,128)(2,1)} %bitcast.118, bf16[4,256,12,64]{1,3,2,0:T(8,128)(2,1)} %bitcast.123), kind=kOutput, calls=%fused_computation.11 | convolution fusion | flops 830447616 | bytes 30507008 | tf_op jit(solution)/shard_map/bqhe,bkhe->bhqk/dot_general | solution.py:46
  123.0 7.2 all-gather
  130.1 11.7 %exponential_reduce_fusion = f32[4,12,512]{2,1,0:T(8,128)S(1)} fusion(f32[4,12,512,256]{2,3,1,0:T(8,128)} %get-tuple-element.187, f32[4,12,512]{2,1,0:T(8,128)S(1)} %get-tuple-element.186, pred[4,512,256]{1,2,0:T(8,128)(4,1)S(1)} %copy-done.7), kind=kLoop, calls=%fused_computation.10 | loop fusion | flops 31432704 | bytes 25886720 | tf_op jit(solution)/shard_map/reduce_sum | solution.py:105
  142.5 7.5 all-gather.1
  150.8 5.5 while.17
  156.3 21.3 %fusion.11 = f32[4,12,64,512]{3,2,1,0:T(8,128)} fusion(bf16[4,256,12,64]{1,3,2,0:T(8,128)(2,1)} %bitcast.132, f32[4,12,512,256]{2,3,1,0:T(8,128)} %get-tuple-element.187, f32[4,12,512]{2,1,0:T(8,128)} %get-tuple-element.141, f32[4,12,512]{2,1,0:T(8,128)} %get-tuple-element.140, pred[4,512,256]{1,2,0:T(8,128)(4,1)} %broadcast_compare_fusion), kind=kOutput, calls=%fused_computation.28 | convolution fusion | flops 855638016 | bytes 33751040 | tf_op jit(solution)/shard_map/bhqk,bkhe->bqhe/dot_general | solution.py:111
  178.0 57.7 %reduce-scatter.24.cloned.1.call-done = f32[4,128,768]{1,2,0:T(8,128)} async-done(((f32[4,512,768]{1,2,0:T(8,128)}), f32[4,128,768]{1,2,0:T(8,128)}) %reduce-scatter.24.cloned.1.call-update) | async-done | bytes 1572880 | tf_op jit(solution)/shard_map/reduce_scatter | solution.py:115
  235.7 3.0 fusion.56
  239.1 4.9 fusion.19
  244.1 6.2 fusion.8
  250.3 3.5 multiply_reduce_fusion.1
  259.1 28.1 %all-gather.13.cloned.1.call-done = bf16[4,512,768]{2,1,0:T(8,128)(2,1)} async-done(((bf16[4,128,768]{2,1,0:T(8,128)(2,1)}), bf16[4,512,768]{2,1,0:T(8,128)(2,1)}) %all-gather.13.cloned.1.call-update) | async-done | bytes 3145744 | tf_op jit(solution)/shard_map/all_gather | solution.py:141
  287.3 4.7 copy.71
  291.9 27.0 %multiply_reduce_fusion = (f32[4,12,512]{2,1,0:T(8,128)}, f32[4,12,512,256]{2,3,1,0:T(8,128)}) fusion(f32[4,12,512]{2,1,0:T(8,128)} %get-tuple-element.141, f32[4,12,512]{2,1,0:T(8,128)} %get-tuple-element.140, pred[4,512,256]{1,2,0:T(8,128)(4,1)} %broadcast_compare_fusion, f32[4,12,512,256]{2,3,1,0:T(8,128)} %get-tuple-element.187, ...), kind=kOutput, calls=%fused_computation.8 | convolution fusion | flops 861904896 | bytes 55869440 | tf_op jit(solution)/shard_map/bqhe,bkhe->bhqk/dot_general | solution.py:146
  319.2 31.7 %all-reduce.2.cloned.1.call-done = f32[4,12,512]{2,1,0:T(8,128)} async-done(((f32[4,12,512]{2,1,0:T(8,128)}), f32[4,12,512]{2,1,0:T(8,128)}) %all-reduce.2.cloned.1.call-update) | async-done | bytes 98320 | tf_op jit(solution)/shard_map/psum | solution.py:149
  350.9 21.8 %multiply_convert_fusion = bf16[4,12,512,256]{2,3,1,0:T(8,128)(2,1)S(1)} fusion(f32[4,12,512,256]{2,3,1,0:T(8,128)} %get-tuple-element.192, f32[4,12,512,256]{2,3,1,0:T(8,128)} %get-tuple-element.187, f32[4,12,512]{2,1,0:T(8,128)} %all-reduce.2.cloned.1.call-done, f32[4,12,512]{2,1,0:T(8,128)} %get-tuple-element.141, f32[4,12,512]{2,1,0:T(8,128)} %get-tuple-element.140, ...), kind=kLoop, calls=%fused_computation.7 | loop fusion | flops 69206016 | bytes 63733760 | tf_op jit(solution)/shard_map/convert_element_type | solution.py:152
  372.7 4.5 multiply_convert_fusion.1
  378.3 4.7 copy.73
  383.0 10.7 %multiply_convert_fusion.3 = bf16[4,12,64,256]{3,2,1,0:T(8,128)(2,1)} fusion(bf16[4,512,12,64]{1,3,2,0:T(8,128)(2,1)} %bitcast.119, bf16[4,12,512,256]{2,3,1,0:T(8,128)(2,1)} %copy-done.1), kind=kOutput, calls=%fused_computation.42 | convolution fusion | flops 806879232 | bytes 17301504 | tf_op jit(solution)/shard_map/bhqk,bqhe->bkhe/dot_general | solution.py:157
  393.7 2.6 copy.75
  396.5 22.1 %fusion.32 = bf16[4,12,64,256]{3,2,1,0:T(8,128)(2,1)} fusion(bf16[4,512,12,64]{1,3,2,0:T(8,128)(2,1)} %bitcast.131, f32[4,12,512,256]{2,3,1,0:T(8,128)} %get-tuple-element.187, f32[4,12,512]{2,1,0:T(8,128)} %get-tuple-element.141, f32[4,12,512]{2,1,0:T(8,128)} %get-tuple-element.140, pred[4,512,256]{1,2,0:T(8,128)(4,1)} %broadcast_compare_fusion), kind=kOutput, calls=%fused_computation.55 | convolution fusion | flops 856424448 | bytes 30605312 | tf_op jit(solution)/shard_map/bhqk,bqhe->bkhe/dot_general | solution.py:160
  418.7 2.6 copy.77
  421.3 3.4 bitcast_convert_fusion.3
  424.8 8.4 bitcast_convert_fusion
  434.0 7.4 bitcast_convert_fusion.1
  443.7 5.6 reduce-scatter.28.cloned.1.call-done
  451.4 26.3 %reduce-scatter.30.cloned.1.call-done = bf16[4,128,768]{2,1,0:T(8,128)(2,1)} async-done(((bf16[4,256,768]{2,1,0:T(8,128)(2,1)}), bf16[4,128,768]{2,1,0:T(8,128)(2,1)}) %reduce-scatter.30.cloned.1.call-update) | async-done | bytes 786448 | tf_op jit(solution)/shard_map/reduce_scatter | solution.py:176
  479.8 6.0 bitcast_convert_fusion.2
  487.8 21.5 %reduce-scatter.34.cloned.1.call-done = bf16[192,768]{1,0:T(8,128)(2,1)} async-done(((bf16[768,768]{1,0:T(8,128)(2,1)}), bf16[192,768]{1,0:T(8,128)(2,1)}) %reduce-scatter.34.cloned.1.call-update) | async-done | bytes 294928 | tf_op jit(solution)/shard_map/reduce_scatter | solution.py:193
  511.3 4.0 fusion.39
  517.7 77.7 %reduce-scatter.38.cloned.1.call-done = bf16[768,768]{1,0:T(8,128)(2,1)} async-done(((bf16[3072,768]{1,0:T(8,128)(2,1)}), bf16[768,768]{1,0:T(8,128)(2,1)}) %reduce-scatter.38.cloned.1.call-update) | async-done | bytes 1179664 | tf_op jit(solution)/shard_map/reduce_scatter | solution.py:199
  597.9 85.5 %reduce-scatter.36.cloned.1.call-done = bf16[192,3072]{1,0:T(8,128)(2,1)} async-done(((bf16[768,3072]{1,0:T(8,128)(2,1)}), bf16[192,3072]{1,0:T(8,128)(2,1)}) %reduce-scatter.36.cloned.1.call-update) | async-done | bytes 1179664 | tf_op jit(solution)/shard_map/reduce_scatter | solution.py:196
  686.4 66.5 %reduce-scatter.32.cloned.1.call-done = bf16[192,2304]{1,0:T(8,128)(2,1)} async-done(((bf16[768,2304]{1,0:T(8,128)(2,1)}), bf16[192,2304]{1,0:T(8,128)(2,1)}) %reduce-scatter.32.cloned.1.call-update) | async-done | bytes 884752 | tf_op jit(solution)/shard_map/reduce_scatter | solution.py:190
  755.2 9.3 add_convert_fusion.1
  764.5 25.9 %reduce-scatter.42.cloned.1.call-done = bf16[96,192]{1,0:T(8,128)(2,1)} async-done(((bf16[768,192]{1,0:T(8,128)(2,1)}), bf16[96,192]{1,0:T(8,128)(2,1)}) %reduce-scatter.42.cloned.1.call-update) | async-done | bytes 36880
  794.1 3.9 add_convert_fusion
  798.0 29.6 %reduce-scatter.48.cloned.1.call-done = bf16[96,4]{1,0:T(8,128)(2,1)} async-done(((bf16[768,4]{1,0:T(8,128)(2,1)}), bf16[96,4]{1,0:T(8,128)(2,1)}) %reduce-scatter.48.cloned.1.call-update) | async-done | bytes 784
  828.4 12.2 %psum.15 = f32[4,96]{1,0:T(4,128)} all-reduce(bf16[4,96]{1,0:T(4,128)(2,1)S(1)} %copy.99), channel_id=1, replica_groups=mesh['batch'=4,'pb'=2,'ka'=4] {'batch'}, use_global_device_ids=true, to_apply=%region_31.32 | all-reduce | flops 384 | bytes 2304 | tf_op jit(solution)/shard_map/psum | solution.py:220
  840.6 26.7 %reduce-scatter.46.cloned.1.call-done = bf16[96,768]{1,0:T(8,128)(2,1)} async-done(((bf16[768,768]{1,0:T(8,128)(2,1)}), bf16[96,768]{1,0:T(8,128)(2,1)}) %reduce-scatter.46.cloned.1.call-update) | async-done | bytes 147472
  870.9 38.0 %reduce-scatter.44.cloned.1.call-done = bf16[384,192]{1,0:T(8,128)(2,1)} async-done(((bf16[3072,192]{1,0:T(8,128)(2,1)}), bf16[384,192]{1,0:T(8,128)(2,1)}) %reduce-scatter.44.cloned.1.call-update) | async-done | bytes 147472
  912.2 36.4 %reduce-scatter.40.cloned.1.call-done = bf16[288,192]{1,0:T(8,128)(2,1)} async-done(((bf16[2304,192]{1,0:T(8,128)(2,1)}), bf16[288,192]{1,0:T(8,128)(2,1)}) %reduce-scatter.40.cloned.1.call-update) | async-done | bytes 110608
  (187 shorter events, 59.7 us)
Async XLA Ops:
  7.2 3.6 copy-start
  7.2 38.5 %all-gather.11.cloned.1.call-start = ((), (), s32[]{:S(2)}) async-start(), calls=%async_computation.15 | async-start | bytes 2359296 | tf_op jit(solution)/shard_map/all_gather | solution.py:96
  8.7 5.4 copy-start.13
  10.8 3.3 copy-start.15
  15.6 58.8 %all-gather.7.cloned.1.call-start = ((), (), s32[]{:S(2)}) async-start(), calls=%async_computation.13 | async-start | bytes 2359296 | tf_op jit(solution)/shard_map/all_gather | solution.py:97
  16.4 88.8 %all-gather.9.cloned.1.call-start = ((), (), s32[]{:S(2)}) async-start(), calls=%async_computation.14 | async-start | bytes 3932160 | tf_op jit(solution)/shard_map/all_gather | solution.py:94
  17.1 218.6 %reduce-scatter.24.cloned.1.call-start = ((), (), s32[]{:S(2)}) async-start(), calls=%async_computation.16 | async-start | bytes 7864320 | tf_op jit(solution)/shard_map/reduce_scatter | solution.py:115
  109.9 20.3 %copy-start.7 = (pred[4,512,256]{1,2,0:T(8,128)(4,1)S(1)}, pred[4,512,256]{1,2,0:T(8,128)(4,1)}, u32[]{:S(2)}) copy-start(pred[4,512,256]{1,2,0:T(8,128)(4,1)} %broadcast_compare_fusion) | copy-start | bytes 1572868
  130.1 11.7 %copy-start.8 = (f32[16,12,512]{2,1,0:T(8,128)}, f32[16,12,512]{2,1,0:T(8,128)S(1)}, u32[]{:S(2)}) copy-start(f32[16,12,512]{2,1,0:T(8,128)S(1)} %all-gather) | copy-start | bytes 1179652
  177.6 61.4 %copy-start.30 = (f32[768]{0:T(1024)S(1)}, f32[768]{0:T(1024)}, u32[]{:S(2)}) copy-start(f32[768]{0:T(1024)} %param.19) | copy-start | bytes 9220
  177.7 61.4 %copy-start.34 = (f32[768]{0:T(1024)S(1)}, f32[768]{0:T(1024)}, u32[]{:S(2)}) copy-start(f32[768]{0:T(1024)} %param.20) | copy-start | bytes 9220
  177.7 109.6 %all-gather.13.cloned.1.call-start = ((), (), s32[]{:S(2)}) async-start(), calls=%async_computation.17 | async-start | bytes 3932160 | tf_op jit(solution)/shard_map/all_gather | solution.py:141
  235.7 8.4 slice-start.2
  238.7 15.2 %copy-start.3 = (f32[4,128,768]{2,1,0:T(8,128)}, f32[4,128,768]{2,1,0:T(8,128)S(1)}, u32[]{:S(2)}) copy-start(f32[4,128,768]{2,1,0:T(8,128)S(1)} %get-tuple-element.189) | copy-start | bytes 4718596
  238.7 15.2 %copy-start.18 = (f32[4,128]{1,0:T(4,128)}, f32[4,128]{1,0:T(4,128)S(1)}, u32[]{:S(2)}) copy-start(f32[4,128]{1,0:T(4,128)S(1)} %broadcast_multiply_fusion) | copy-start | bytes 6148
  239.1 14.8 %copy-start.28 = (f32[4,128]{1,0:T(4,128)}, f32[4,128]{1,0:T(4,128)S(1)}, u32[]{:S(2)}) copy-start(f32[4,128]{1,0:T(4,128)S(1)} %fusion.51) | copy-start | bytes 6148
  239.1 5.0 copy-start.11
  239.1 5.0 slice-start.3
  239.1 11.2 %slice-start = ((s8[4718592]{0:T(1024)(128)(4,1)}), s8[4194304]{0:T(1024)(128)(4,1)S(1)}, s32[]{:S(2)}) async-start(s8[4718592]{0:T(1024)(128)(4,1)} %bitcast.142), calls=%async_computation.31 | async-start | bytes 8388608
  244.1 6.2 copy-start.37
  244.1 6.2 slice-start.1
  250.3 3.5 copy-start.38
  258.6 92.3 %all-reduce.2.cloned.1.call-start = ((), (), s32[]{:S(2)}) async-start(), calls=%async_computation.18 | async-start | bytes 262144 | tf_op jit(solution)/shard_map/psum | solution.py:149
  319.0 122.5 %reduce-scatter.26.cloned.1.call-start = ((), (), s32[]{:S(2)}) async-start(), calls=%async_computation.19 | async-start | bytes 3932160 | tf_op jit(solution)/shard_map/reduce_scatter | solution.py:163
  350.9 21.8 %copy-start.5 = (bf16[4,256,768]{1,2,0:T(8,128)(2,1)S(1)}, bf16[4,256,768]{1,2,0:T(8,128)(2,1)}, u32[]{:S(2)}) copy-start(bf16[4,256,768]{1,2,0:T(8,128)(2,1)} %copy.64) | copy-start | bytes 4718596
  372.7 5.5 copy-start.1
  382.9 66.3 %reduce-scatter.28.cloned.1.call-start = ((), (), s32[]{:S(2)}) async-start(), calls=%async_computation.20 | async-start | bytes 2359296 | tf_op jit(solution)/shard_map/reduce_scatter | solution.py:170
  396.3 81.4 %reduce-scatter.30.cloned.1.call-start = ((), (), s32[]{:S(2)}) async-start(), calls=%async_computation.21 | async-start | bytes 2359296 | tf_op jit(solution)/shard_map/reduce_scatter | solution.py:176
  421.3 88.0 %reduce-scatter.34.cloned.1.call-start = ((), (), s32[]{:S(2)}) async-start(), calls=%async_computation.23 | async-start | bytes 1474560 | tf_op jit(solution)/shard_map/reduce_scatter | solution.py:193
  424.8 170.7 %reduce-scatter.38.cloned.1.call-start = ((), (), s32[]{:S(2)}) async-start(), calls=%async_computation.25 | async-start | bytes 5898240 | tf_op jit(solution)/shard_map/reduce_scatter | solution.py:199
  433.3 250.2 %reduce-scatter.36.cloned.1.call-start = ((), (), s32[]{:S(2)}) async-start(), calls=%async_computation.24 | async-start | bytes 5898240 | tf_op jit(solution)/shard_map/reduce_scatter | solution.py:196
  441.4 38.4 %copy-start.14 = (f32[4,128]{1,0:T(4,128)S(1)}, f32[4,128]{1,0:T(4,128)}, u32[]{:S(2)}) copy-start(f32[4,128]{1,0:T(4,128)} %copy-done.13) | copy-start | bytes 6148
  441.4 38.4 %copy-start.16 = (f32[4,128]{1,0:T(4,128)S(1)}, f32[4,128]{1,0:T(4,128)}, u32[]{:S(2)}) copy-start(f32[4,128]{1,0:T(4,128)} %copy-done.15) | copy-start | bytes 6148
  441.4 38.4 %copy-start.24 = (f32[768]{0:T(1024)S(1)}, f32[768]{0:T(1024)}, u32[]{:S(2)}) copy-start(f32[768]{0:T(1024)} %param.15) | copy-start | bytes 9220
  441.4 38.4 %copy-start.36 = (f32[768]{0:T(1024)S(1)}, f32[768]{0:T(1024)}, u32[]{:S(2)}) copy-start(f32[768]{0:T(1024)} %param.16) | copy-start | bytes 9220
  441.4 311.5 %reduce-scatter.32.cloned.1.call-start = ((), (), s32[]{:S(2)}) async-start(), calls=%async_computation.22 | async-start | bytes 4423680 | tf_op jit(solution)/shard_map/reduce_scatter | solution.py:190
  485.9 304.6 %reduce-scatter.42.cloned.1.call-start = ((), (), s32[]{:S(2)}) async-start(), calls=%async_computation.27 | async-start | bytes 442368
  511.2 4.1 copy-start.21
  511.2 316.4 %reduce-scatter.48.cloned.1.call-start = ((), (), s32[]{:S(2)}) async-start(), calls=%async_computation.30 | async-start | bytes 221184
  511.2 4.1 copy-start.2
  511.2 4.1 copy-start.25
  511.3 5.5 copy-start.26
  511.3 5.5 copy-start.27
  517.7 349.7 %reduce-scatter.46.cloned.1.call-start = ((), (), s32[]{:S(2)}) async-start(), calls=%async_computation.29 | async-start | bytes 1327104
  597.9 310.9 %reduce-scatter.44.cloned.1.call-start = ((), (), s32[]{:S(2)}) async-start(), calls=%async_computation.28 | async-start | bytes 1769472
  686.0 262.6 %reduce-scatter.40.cloned.1.call-start = ((), (), s32[]{:S(2)}) async-start(), calls=%async_computation.26 | async-start | bytes 1327104
  755.2 38.9 %copy-start.17 = (f32[4,128]{1,0:T(4,128)S(1)}, f32[4,128]{1,0:T(4,128)}, u32[]{:S(2)}) copy-start(f32[4,128]{1,0:T(4,128)} %copy-done.15) | copy-start | bytes 6148
  755.2 38.9 %copy-start.23 = (f32[4,128]{1,0:T(4,128)S(1)}, f32[4,128]{1,0:T(4,128)}, u32[]{:S(2)}) copy-start(f32[4,128]{1,0:T(4,128)} %copy-done.22) | copy-start | bytes 6148
  (13 other events, 16.5 us)
Sparse Core Ops, SparseCore 0:
  15.8 29.8 all-gather.10
  47.2 27.1 all-gather.6
  76.6 28.5 all-gather.8
  177.8 57.8 reduce-scatter.23
  258.7 28.4 all-gather.12
  319.1 31.7 all-reduce.1
  383.1 37.7 reduce-scatter.25
  423.1 26.1 reduce-scatter.27
  451.5 26.1 reduce-scatter.29
  479.9 29.3 reduce-scatter.33
  511.6 83.8 reduce-scatter.37
  597.6 85.7 reduce-scatter.35
  685.8 67.0 reduce-scatter.31
  756.4 34.0 reduce-scatter.41
  793.9 33.6 reduce-scatter.47
  830.6 36.6 reduce-scatter.45
  870.5 38.2 reduce-scatter.43
  911.9 36.6 reduce-scatter.39
where the time goes:
time: 967 us; the launch traced here: 959 us
  waiting for transfers between devices  639 us (66%)
  matrix products  160 us (17%)
  local copies, waits for them, and re-layouts  60.4 us (6%)
  other arithmetic  55.3 us (6%)
  blocking collectives  26.9 us (3%)
  between operations  15.4 us (2%)
    unnamed x23, waiting for transfers between devices  158 us
    reduce_scatter x1, waiting for transfers between devices, shards(): lax.psum_scatter(grad_up.astype(jnp.bfloat16), 'batch', scatter_dimension...  85.5 us
    reduce_scatter x1, waiting for transfers between devices, shards(): lax.psum_scatter(grad_down.astype(jnp.bfloat16), 'batch', scatter_dimensi...  77.7 us
    reduce_scatter x1, waiting for transfers between devices, shards(): lax.psum_scatter(grad_qkv.astype(jnp.bfloat16), 'batch', scatter_dimensio...  66.5 us
    reduce_scatter x1, waiting for transfers between devices, shards(): lax.psum_scatter(partial_value, 'ka', scatter_dimension=1, tiled=True)  57.7 us
    psum x1, waiting for transfers between devices, shards(): delta_rows = lax.psum(jnp.sum(signed * grad_weights, axis=-1), 'ka')  31.7 us
    all_gather x1, waiting for transfers between devices, shards(): grad_half = lax.all_gather(grad_att, 'ka', axis=1, tiled=True)  28.1 us
    all_gather x1, waiting for transfers between devices, shards(): lax.all_gather(packed[..., :model_width], 'ka', axis=1, tiled=True)  28.1 us
  transfers between devices with their start and end apart: 18, of which 17 were waited for; matrix products, arithmetic and copies ran while one was open for 12% of the time, Pallas kernels for 0%

commit v1 on v0

--- a/solution.py
+++ b/solution.py
@@ -146,7 +146,9 @@
     grad_weights = jnp.einsum(
         "bqhe,bkhe->bhqk", grad_heads, value_heads, preferred_element_type=jnp.float32
     )
-    delta_rows = lax.psum(jnp.sum(signed * grad_weights, axis=-1), "ka")
+    own = jnp.sum(signed * grad_weights, axis=-1)
+    parts = lax.all_gather(own, "ka", axis=0, tiled=False)
+    delta_rows = parts.sum(axis=0)
     grad_scores = (
         sign_part * prob_part * (sign_part * grad_weights - delta_rows[..., None])
     ).astype(jnp.bfloat16)

time: 967 us -> 946 us (0.978)
  waiting for transfers between devices: 639 us -> 609 us
    psum x1 -> x0, waiting for transfers between devices: 31.7 us -> none  [shards(): delta_rows = lax.psum(jnp.sum(signed * grad_weights, axis=-1), 'ka')]
    unnamed x23 -> x22, waiting for transfers between devices: 158 us -> 159 us
  transfers between devices with their start and end apart: 18 -> 17, of which waited for: 17 -> 16; matrix products, arithmetic and copies ran while one was open for 12% -> 13% of each run, Pallas kernels for 0% -> 0%
where the time goes in v1:
time: 946 us; the launch traced here: 938 us
  waiting for transfers between devices  609 us (64%)
  matrix products  160 us (17%)
  local copies, waits for them, and re-layouts  60.4 us (6%)
  other arithmetic  57 us (6%)
  blocking collectives  34.9 us (4%)
  between operations  15.1 us (2%)
    unnamed x22, waiting for transfers between devices  159 us
    reduce_scatter x1, waiting for transfers between devices, shards(): lax.psum_scatter(grad_up.astype(jnp.bfloat16), 'batch', scatter_dimension...  85.7 us
    reduce_scatter x1, waiting for transfers between devices, shards(): lax.psum_scatter(grad_down.astype(jnp.bfloat16), 'batch', scatter_dimensi...  77.6 us
    reduce_scatter x1, waiting for transfers between devices, shards(): lax.psum_scatter(grad_qkv.astype(jnp.bfloat16), 'batch', scatter_dimensio...  66.4 us
    reduce_scatter x1, waiting for transfers between devices, shards(): lax.psum_scatter(partial_value, 'ka', scatter_dimension=1, tiled=True)  57.7 us
    all_gather x1, waiting for transfers between devices, shards(): grad_half = lax.all_gather(grad_att, 'ka', axis=1, tiled=True)  28.2 us
    all_gather x1, waiting for transfers between devices, shards(): lax.all_gather(packed[..., :model_width], 'ka', axis=1, tiled=True)  28.1 us
    unnamed x102, local copies, waits for them, and re-layouts  27.9 us
  transfers between devices with their start and end apart: 17, of which 16 were waited for; matrix products, arithmetic and copies ran while one was open for 13% of the time, Pallas kernels for 0%

profile of v1, /device:TPU:0, one launch (start us, length us, event | category | flops | bytes accessed | tf_op | source)
XLA Modules:
  0.0 938.1 jit_solution(15462200426140176571)
XLA Ops:
  10.8 3.3 convolution_convert_fusion
  20.1 25.6 %all-gather.12.cloned.1.call-done = bf16[4,256,768]{2,1,0:T(8,128)(2,1)} async-done(((bf16[4,128,768]{2,1,0:T(8,128)(2,1)}), bf16[4,256,768]{2,1,0:T(8,128)(2,1)}) %all-gather.12.cloned.1.call-update) | async-done | bytes 1572880 | tf_op jit(solution)/shard_map/all_gather | solution.py:96
  45.7 2.6 copy.64
  48.3 26.2 %all-gather.8.cloned.1.call-done = bf16[4,256,768]{2,1,0:T(8,128)(2,1)} async-done(((bf16[4,128,768]{2,1,0:T(8,128)(2,1)}), bf16[4,256,768]{2,1,0:T(8,128)(2,1)}) %all-gather.8.cloned.1.call-update) | async-done | bytes 1572880 | tf_op jit(solution)/shard_map/all_gather | solution.py:97
  74.5 2.6 copy.62
  77.1 28.1 %all-gather.10.cloned.1.call-done = bf16[4,512,768]{2,1,0:T(8,128)(2,1)} async-done(((bf16[4,128,768]{2,1,0:T(8,128)(2,1)}), bf16[4,512,768]{2,1,0:T(8,128)(2,1)}) %all-gather.10.cloned.1.call-update) | async-done | bytes 3145744 | tf_op jit(solution)/shard_map/all_gather | solution.py:94
  105.2 4.7 copy.63
  109.8 13.1 %select_reduce_fusion = (f32[4,12,512]{2,1,0:T(8,128)S(1)}, f32[4,12,512,256]{2,3,1,0:T(8,128)}) fusion(pred[4,512,256]{1,2,0:T(8,128)(4,1)} %broadcast_compare_fusion, bf16[4,512,12,64]{1,3,2,0:T(8,128)(2,1)} %bitcast.119, bf16[4,256,12,64]{1,3,2,0:T(8,128)(2,1)} %bitcast.124), kind=kOutput, calls=%fused_computation.11 | convolution fusion | flops 830447616 | bytes 30507008 | tf_op jit(solution)/shard_map/bqhe,bkhe->bhqk/dot_general | solution.py:46
  122.9 7.2 all-gather
  130.1 11.7 %exponential_reduce_fusion = f32[4,12,512]{2,1,0:T(8,128)S(1)} fusion(f32[4,12,512,256]{2,3,1,0:T(8,128)} %get-tuple-element.187, f32[4,12,512]{2,1,0:T(8,128)S(1)} %get-tuple-element.186, pred[4,512,256]{1,2,0:T(8,128)(4,1)S(1)} %copy-done.7), kind=kLoop, calls=%fused_computation.10 | loop fusion | flops 31432704 | bytes 25886720 | tf_op jit(solution)/shard_map/reduce_sum | solution.py:105
  142.4 7.5 all-gather.1
  150.7 5.5 while.17
  156.2 21.3 %fusion.11 = f32[4,12,64,512]{3,2,1,0:T(8,128)} fusion(bf16[4,256,12,64]{1,3,2,0:T(8,128)(2,1)} %bitcast.134, f32[4,12,512,256]{2,3,1,0:T(8,128)} %get-tuple-element.187, f32[4,12,512]{2,1,0:T(8,128)} %get-tuple-element.141, f32[4,12,512]{2,1,0:T(8,128)} %get-tuple-element.140, pred[4,512,256]{1,2,0:T(8,128)(4,1)} %broadcast_compare_fusion), kind=kOutput, calls=%fused_computation.28 | convolution fusion | flops 855638016 | bytes 33751040 | tf_op jit(solution)/shard_map/bhqk,bkhe->bqhe/dot_general | solution.py:111
  177.9 57.7 %reduce-scatter.24.cloned.1.call-done = f32[4,128,768]{1,2,0:T(8,128)} async-done(((f32[4,512,768]{1,2,0:T(8,128)}), f32[4,128,768]{1,2,0:T(8,128)}) %reduce-scatter.24.cloned.1.call-update) | async-done | bytes 1572880 | tf_op jit(solution)/shard_map/reduce_scatter | solution.py:115
  235.6 3.0 fusion.56
  239.1 4.9 fusion.19
  244.1 6.2 fusion.8
  250.3 3.5 multiply_reduce_fusion.1
  259.1 28.2 %all-gather.14.cloned.1.call-done = bf16[4,512,768]{2,1,0:T(8,128)(2,1)} async-done(((bf16[4,128,768]{2,1,0:T(8,128)(2,1)}), bf16[4,512,768]{2,1,0:T(8,128)(2,1)}) %all-gather.14.cloned.1.call-update) | async-done | bytes 3145744 | tf_op jit(solution)/shard_map/all_gather | solution.py:141
  287.2 4.6 copy.71
  291.9 27.0 %multiply_reduce_fusion = (f32[4,12,512]{2,1,0:T(8,128)}, f32[4,12,512,256]{2,3,1,0:T(8,128)}) fusion(f32[4,12,512]{2,1,0:T(8,128)} %get-tuple-element.141, f32[4,12,512]{2,1,0:T(8,128)} %get-tuple-element.140, pred[4,512,256]{1,2,0:T(8,128)(4,1)} %broadcast_compare_fusion, f32[4,12,512,256]{2,3,1,0:T(8,128)} %get-tuple-element.187, ...), kind=kOutput, calls=%fused_computation.8 | convolution fusion | flops 861904896 | bytes 55869440 | tf_op jit(solution)/shard_map/bqhe,bkhe->bhqk/dot_general | solution.py:146
  318.9 8.1 all-gather.2
  328.7 21.8 %multiply_convert_fusion = bf16[4,12,512,256]{2,3,1,0:T(8,128)(2,1)S(1)} fusion(f32[4,12,512,256]{2,3,1,0:T(8,128)} %get-tuple-element.192, f32[4,12,512,256]{2,3,1,0:T(8,128)} %get-tuple-element.187, f32[4,12,512]{2,1,0:T(8,128)} %reduce_sum.146, f32[4,12,512]{2,1,0:T(8,128)} %get-tuple-element.141, f32[4,12,512]{2,1,0:T(8,128)} %get-tuple-element.140, ...), kind=kLoop, calls=%fused_computation.7 | loop fusion | flops 69206016 | bytes 63733760 | tf_op jit(solution)/shard_map/convert_element_type | solution.py:154
  350.6 4.5 multiply_convert_fusion.1
  356.1 4.6 copy.73
  360.8 10.6 %multiply_convert_fusion.3 = bf16[4,12,64,256]{3,2,1,0:T(8,128)(2,1)} fusion(bf16[4,512,12,64]{1,3,2,0:T(8,128)(2,1)} %bitcast.120, bf16[4,12,512,256]{2,3,1,0:T(8,128)(2,1)} %copy-done.1), kind=kOutput, calls=%fused_computation.42 | convolution fusion | flops 806879232 | bytes 17301504 | tf_op jit(solution)/shard_map/bhqk,bqhe->bkhe/dot_general | solution.py:159
  371.4 2.6 copy.75
  374.3 21.9 %fusion.32 = bf16[4,12,64,256]{3,2,1,0:T(8,128)(2,1)} fusion(bf16[4,512,12,64]{1,3,2,0:T(8,128)(2,1)} %bitcast.132, f32[4,12,512,256]{2,3,1,0:T(8,128)} %get-tuple-element.187, f32[4,12,512]{2,1,0:T(8,128)} %get-tuple-element.141, f32[4,12,512]{2,1,0:T(8,128)} %get-tuple-element.140, pred[4,512,256]{1,2,0:T(8,128)(4,1)} %broadcast_compare_fusion), kind=kOutput, calls=%fused_computation.55 | convolution fusion | flops 856424448 | bytes 30605312 | tf_op jit(solution)/shard_map/bhqk,bqhe->bkhe/dot_general | solution.py:162
  396.2 2.6 copy.77
  398.9 3.5 bitcast_convert_fusion.3
  402.4 8.4 bitcast_convert_fusion
  411.6 7.4 bitcast_convert_fusion.1
  421.2 7.0 reduce-scatter.28.cloned.1.call-done
  430.4 26.3 %reduce-scatter.30.cloned.1.call-done = bf16[4,128,768]{2,1,0:T(8,128)(2,1)} async-done(((bf16[4,256,768]{2,1,0:T(8,128)(2,1)}), bf16[4,128,768]{2,1,0:T(8,128)(2,1)}) %reduce-scatter.30.cloned.1.call-update) | async-done | bytes 786448 | tf_op jit(solution)/shard_map/reduce_scatter | solution.py:178
  458.8 6.0 bitcast_convert_fusion.2
  466.7 21.6 %reduce-scatter.34.cloned.1.call-done = bf16[192,768]{1,0:T(8,128)(2,1)} async-done(((bf16[768,768]{1,0:T(8,128)(2,1)}), bf16[192,768]{1,0:T(8,128)(2,1)}) %reduce-scatter.34.cloned.1.call-update) | async-done | bytes 294928 | tf_op jit(solution)/shard_map/reduce_scatter | solution.py:195
  490.3 4.0 fusion.39
  496.8 77.6 %reduce-scatter.38.cloned.1.call-done = bf16[768,768]{1,0:T(8,128)(2,1)} async-done(((bf16[3072,768]{1,0:T(8,128)(2,1)}), bf16[768,768]{1,0:T(8,128)(2,1)}) %reduce-scatter.38.cloned.1.call-update) | async-done | bytes 1179664 | tf_op jit(solution)/shard_map/reduce_scatter | solution.py:201
  576.8 85.7 %reduce-scatter.36.cloned.1.call-done = bf16[192,3072]{1,0:T(8,128)(2,1)} async-done(((bf16[768,3072]{1,0:T(8,128)(2,1)}), bf16[192,3072]{1,0:T(8,128)(2,1)}) %reduce-scatter.36.cloned.1.call-update) | async-done | bytes 1179664 | tf_op jit(solution)/shard_map/reduce_scatter | solution.py:198
  665.4 66.4 %reduce-scatter.32.cloned.1.call-done = bf16[192,2304]{1,0:T(8,128)(2,1)} async-done(((bf16[768,2304]{1,0:T(8,128)(2,1)}), bf16[192,2304]{1,0:T(8,128)(2,1)}) %reduce-scatter.32.cloned.1.call-update) | async-done | bytes 884752 | tf_op jit(solution)/shard_map/reduce_scatter | solution.py:192
  734.1 9.3 add_convert_fusion.1
  743.4 26.1 %reduce-scatter.42.cloned.1.call-done = bf16[96,192]{1,0:T(8,128)(2,1)} async-done(((bf16[768,192]{1,0:T(8,128)(2,1)}), bf16[96,192]{1,0:T(8,128)(2,1)}) %reduce-scatter.42.cloned.1.call-update) | async-done | bytes 36880
  773.1 3.9 add_convert_fusion
  777.0 29.6 %reduce-scatter.48.cloned.1.call-done = bf16[96,4]{1,0:T(8,128)(2,1)} async-done(((bf16[768,4]{1,0:T(8,128)(2,1)}), bf16[96,4]{1,0:T(8,128)(2,1)}) %reduce-scatter.48.cloned.1.call-update) | async-done | bytes 784
  807.4 12.2 %psum.7 = f32[4,96]{1,0:T(4,128)} all-reduce(bf16[4,96]{1,0:T(4,128)(2,1)S(1)} %copy.99), channel_id=1, replica_groups=mesh['batch'=4,'pb'=2,'ka'=4] {'batch'}, use_global_device_ids=true, to_apply=%region_31.32 | all-reduce | flops 384 | bytes 2304 | tf_op jit(solution)/shard_map/psum | solution.py:222
  819.6 26.8 %reduce-scatter.46.cloned.1.call-done = bf16[96,768]{1,0:T(8,128)(2,1)} async-done(((bf16[768,768]{1,0:T(8,128)(2,1)}), bf16[96,768]{1,0:T(8,128)(2,1)}) %reduce-scatter.46.cloned.1.call-update) | async-done | bytes 147472
  849.9 38.1 %reduce-scatter.44.cloned.1.call-done = bf16[384,192]{1,0:T(8,128)(2,1)} async-done(((bf16[3072,192]{1,0:T(8,128)(2,1)}), bf16[384,192]{1,0:T(8,128)(2,1)}) %reduce-scatter.44.cloned.1.call-update) | async-done | bytes 147472
  891.3 36.4 %reduce-scatter.40.cloned.1.call-done = bf16[288,192]{1,0:T(8,128)(2,1)} async-done(((bf16[2304,192]{1,0:T(8,128)(2,1)}), bf16[288,192]{1,0:T(8,128)(2,1)}) %reduce-scatter.40.cloned.1.call-update) | async-done | bytes 110608
  (186 shorter events, 61.2 us)
Async XLA Ops:
  7.2 3.6 copy-start
  7.2 38.5 %all-gather.12.cloned.1.call-start = ((), (), s32[]{:S(2)}) async-start(), calls=%async_computation.15 | async-start | bytes 2359296 | tf_op jit(solution)/shard_map/all_gather | solution.py:96
  8.7 5.4 copy-start.13
  10.8 3.3 copy-start.15
  14.1 3.1 copy-start.32
  15.6 58.8 %all-gather.8.cloned.1.call-start = ((), (), s32[]{:S(2)}) async-start(), calls=%async_computation.13 | async-start | bytes 2359296 | tf_op jit(solution)/shard_map/all_gather | solution.py:97
  16.4 88.8 %all-gather.10.cloned.1.call-start = ((), (), s32[]{:S(2)}) async-start(), calls=%async_computation.14 | async-start | bytes 3932160 | tf_op jit(solution)/shard_map/all_gather | solution.py:94
  17.1 218.5 %reduce-scatter.24.cloned.1.call-start = ((), (), s32[]{:S(2)}) async-start(), calls=%async_computation.16 | async-start | bytes 7864320 | tf_op jit(solution)/shard_map/reduce_scatter | solution.py:115
  109.8 20.2 %copy-start.7 = (pred[4,512,256]{1,2,0:T(8,128)(4,1)S(1)}, pred[4,512,256]{1,2,0:T(8,128)(4,1)}, u32[]{:S(2)}) copy-start(pred[4,512,256]{1,2,0:T(8,128)(4,1)} %broadcast_compare_fusion) | copy-start | bytes 1572868
  130.1 11.7 %copy-start.8 = (f32[16,12,512]{2,1,0:T(8,128)}, f32[16,12,512]{2,1,0:T(8,128)S(1)}, u32[]{:S(2)}) copy-start(f32[16,12,512]{2,1,0:T(8,128)S(1)} %all-gather) | copy-start | bytes 1179652
  177.6 61.4 %copy-start.30 = (f32[768]{0:T(1024)S(1)}, f32[768]{0:T(1024)}, u32[]{:S(2)}) copy-start(f32[768]{0:T(1024)} %param.19) | copy-start | bytes 9220
  177.6 61.4 %copy-start.34 = (f32[768]{0:T(1024)S(1)}, f32[768]{0:T(1024)}, u32[]{:S(2)}) copy-start(f32[768]{0:T(1024)} %param.20) | copy-start | bytes 9220
  177.6 109.6 %all-gather.14.cloned.1.call-start = ((), (), s32[]{:S(2)}) async-start(), calls=%async_computation.17 | async-start | bytes 3932160 | tf_op jit(solution)/shard_map/all_gather | solution.py:141
  235.6 8.4 slice-start.2
  238.7 15.2 %copy-start.3 = (f32[4,128,768]{2,1,0:T(8,128)}, f32[4,128,768]{2,1,0:T(8,128)S(1)}, u32[]{:S(2)}) copy-start(f32[4,128,768]{2,1,0:T(8,128)S(1)} %get-tuple-element.189) | copy-start | bytes 4718596
  238.7 15.2 %copy-start.18 = (f32[4,128]{1,0:T(4,128)}, f32[4,128]{1,0:T(4,128)S(1)}, u32[]{:S(2)}) copy-start(f32[4,128]{1,0:T(4,128)S(1)} %broadcast_multiply_fusion) | copy-start | bytes 6148
  239.0 14.8 %copy-start.28 = (f32[4,128]{1,0:T(4,128)}, f32[4,128]{1,0:T(4,128)S(1)}, u32[]{:S(2)}) copy-start(f32[4,128]{1,0:T(4,128)S(1)} %fusion.51) | copy-start | bytes 6148
  239.0 5.0 copy-start.11
  239.0 5.0 slice-start.3
  239.1 11.2 %slice-start = ((s8[4718592]{0:T(1024)(128)(4,1)}), s8[4194304]{0:T(1024)(128)(4,1)S(1)}, s32[]{:S(2)}) async-start(s8[4718592]{0:T(1024)(128)(4,1)} %bitcast.144), calls=%async_computation.30 | async-start | bytes 8388608
  244.0 6.2 copy-start.37
  244.1 6.2 slice-start.1
  250.3 3.5 copy-start.38
  258.5 160.5 %reduce-scatter.26.cloned.1.call-start = ((), (), s32[]{:S(2)}) async-start(), calls=%async_computation.18 | async-start | bytes 3932160 | tf_op jit(solution)/shard_map/reduce_scatter | solution.py:165
  328.7 21.8 %copy-start.5 = (bf16[4,256,768]{1,2,0:T(8,128)(2,1)S(1)}, bf16[4,256,768]{1,2,0:T(8,128)(2,1)}, u32[]{:S(2)}) copy-start(bf16[4,256,768]{1,2,0:T(8,128)(2,1)} %copy.64) | copy-start | bytes 4718596
  350.6 5.5 copy-start.1
  360.7 67.5 %reduce-scatter.28.cloned.1.call-start = ((), (), s32[]{:S(2)}) async-start(), calls=%async_computation.19 | async-start | bytes 2359296 | tf_op jit(solution)/shard_map/reduce_scatter | solution.py:172
  374.1 82.6 %reduce-scatter.30.cloned.1.call-start = ((), (), s32[]{:S(2)}) async-start(), calls=%async_computation.20 | async-start | bytes 2359296 | tf_op jit(solution)/shard_map/reduce_scatter | solution.py:178
  398.8 89.5 %reduce-scatter.34.cloned.1.call-start = ((), (), s32[]{:S(2)}) async-start(), calls=%async_computation.22 | async-start | bytes 1474560 | tf_op jit(solution)/shard_map/reduce_scatter | solution.py:195
  402.4 172.0 %reduce-scatter.38.cloned.1.call-start = ((), (), s32[]{:S(2)}) async-start(), calls=%async_computation.24 | async-start | bytes 5898240 | tf_op jit(solution)/shard_map/reduce_scatter | solution.py:201
  410.9 251.6 %reduce-scatter.36.cloned.1.call-start = ((), (), s32[]{:S(2)}) async-start(), calls=%async_computation.23 | async-start | bytes 5898240 | tf_op jit(solution)/shard_map/reduce_scatter | solution.py:198
  419.0 39.8 %copy-start.14 = (f32[4,128]{1,0:T(4,128)S(1)}, f32[4,128]{1,0:T(4,128)}, u32[]{:S(2)}) copy-start(f32[4,128]{1,0:T(4,128)} %copy-done.13) | copy-start | bytes 6148
  419.0 39.8 %copy-start.16 = (f32[4,128]{1,0:T(4,128)S(1)}, f32[4,128]{1,0:T(4,128)}, u32[]{:S(2)}) copy-start(f32[4,128]{1,0:T(4,128)} %copy-done.15) | copy-start | bytes 6148
  419.0 39.8 %copy-start.24 = (f32[768]{0:T(1024)S(1)}, f32[768]{0:T(1024)}, u32[]{:S(2)}) copy-start(f32[768]{0:T(1024)} %param.15) | copy-start | bytes 9220
  419.0 39.8 %copy-start.36 = (f32[768]{0:T(1024)S(1)}, f32[768]{0:T(1024)}, u32[]{:S(2)}) copy-start(f32[768]{0:T(1024)} %param.16) | copy-start | bytes 9220
  419.0 312.7 %reduce-scatter.32.cloned.1.call-start = ((), (), s32[]{:S(2)}) async-start(), calls=%async_computation.21 | async-start | bytes 4423680 | tf_op jit(solution)/shard_map/reduce_scatter | solution.py:192
  464.8 304.7 %reduce-scatter.42.cloned.1.call-start = ((), (), s32[]{:S(2)}) async-start(), calls=%async_computation.26 | async-start | bytes 442368
  490.2 4.1 copy-start.21
  490.2 316.4 %reduce-scatter.48.cloned.1.call-start = ((), (), s32[]{:S(2)}) async-start(), calls=%async_computation.29 | async-start | bytes 221184
  490.3 4.1 copy-start.2
  490.3 4.1 copy-start.25
  490.3 5.5 copy-start.26
  490.3 5.5 copy-start.27
  496.7 349.6 %reduce-scatter.46.cloned.1.call-start = ((), (), s32[]{:S(2)}) async-start(), calls=%async_computation.28 | async-start | bytes 1327104
  576.8 311.2 %reduce-scatter.44.cloned.1.call-start = ((), (), s32[]{:S(2)}) async-start(), calls=%async_computation.27 | async-start | bytes 1769472
  665.1 262.7 %reduce-scatter.40.cloned.1.call-start = ((), (), s32[]{:S(2)}) async-start(), calls=%async_computation.25 | async-start | bytes 1327104
  734.1 39.0 %copy-start.17 = (f32[4,128]{1,0:T(4,128)S(1)}, f32[4,128]{1,0:T(4,128)}, u32[]{:S(2)}) copy-start(f32[4,128]{1,0:T(4,128)} %copy-done.15) | copy-start | bytes 6148
  734.1 39.0 %copy-start.23 = (f32[4,128]{1,0:T(4,128)S(1)}, f32[4,128]{1,0:T(4,128)}, u32[]{:S(2)}) copy-start(f32[4,128]{1,0:T(4,128)} %copy-done.22) | copy-start | bytes 6148
  (12 other events, 13.5 us)
Sparse Core Ops, SparseCore 0:
  15.8 29.8 all-gather.11
  47.2 27.1 all-gather.7
  76.6 28.5 all-gather.9
  177.7 57.8 reduce-scatter.23
  258.7 28.5 all-gather.13
  360.9 38.8 reduce-scatter.25
  402.0 26.1 reduce-scatter.27
  430.4 26.1 reduce-scatter.29
  458.9 29.3 reduce-scatter.33
  490.4 83.8 reduce-scatter.37
  576.7 85.7 reduce-scatter.35
  664.7 67.0 reduce-scatter.31
  735.4 34.0 reduce-scatter.41
  772.9 33.6 reduce-scatter.47
  809.7 36.6 reduce-scatter.45
  849.5 38.3 reduce-scatter.43
  891.0 36.6 reduce-scatter.39
